TPU v7x, 256 devices: a whole 4x4x8 slice. The times are simulated.
256 devices in a mesh: row: 8 (over x, core), col: 32 (over z, y).
Axes of the slice: x: 4, y: 4, z: 8, core: 2. Of those that a mesh axis runs over, the one named last changes fastest.
Arguments:
- layer_input: bfloat16 [16896, 1024], P('col', 'row'), may hold values from -6 to 6
- w_q: bfloat16 [1024, 1024], P('col', 'row'), may hold values from -0.1875 to 0.1875
- w_k: bfloat16 [1024, 1024], P('col', 'row'), may hold values from -0.1875 to 0.1875
- w_v: bfloat16 [1024, 1024], P('col', 'row'), may hold values from -0.1875 to 0.1875
- w_o: bfloat16 [1024, 1024], P('row', 'col'), may hold values from -0.375 to 0.375
- w_gate: bfloat16 [1024, 4096], P('col', 'row'), may hold values from -0.1875 to 0.1875
- w_up: bfloat16 [1024, 4096], P('col', 'row'), may hold values from -0.1875 to 0.1875
- w_down: bfloat16 [4096, 1024], P('row', 'col'), may hold values from -0.1875 to 0.1875
- norm1: float32 [1024], replicated, may hold values from 0.5 to 1.5
- norm2: float32 [1024], replicated, may hold values from 0.5 to 1.5
- q_gain: float32 [1024], P('row'), may hold values from 0.5 to 1.5
- k_gain: float32 [1024], P('row'), may hold values from 0.5 to 1.5
- bias_same: float32 [16], P('row'), may hold values from -3 to 3
- bias_diff: float32 [16], P('row'), may hold values from -3 to 3
- pre_variate: int32 [32, 512], P('col'), may hold values from 0 to 7, never falling along the last dimension, each value on 1 to 128 neighbouring positions
- pre_keep: int32 [32, 512], P('col'), may hold values 0 or 1
- dec_variate: int32 [512], P('col'), may hold values from 0 to 7
- dec_len: int32 [512], P('col'), may hold values from 1 to 1023, as said below
- dec_table: int32 [512, 8], P('col'), may hold values from 0 to 31
- dec_holder: int32 [512, 1], P('col'), may hold values from 0 to 31; in each aligned block of 16 rows (0 to 15, 16 to 31, ...) at most 2 rows name the same one
- kv_pool: bfloat16 [1024, 2, 128, 1024], P('col', None, None, 'row'), may hold values from -4 to 4
- page_variates: int32 [1024, 128], P('col'), may hold values from 0 to 7
Outputs:
- hidden: bfloat16 [16896, 1024], P('col', 'row')
- prefill_pages: bfloat16 [128, 2, 128, 1024], P('col', None, None, 'row')
- tail_pages: bfloat16 [512, 2, 128, 1024], P('col', None, None, 'row')
Inputs may be any that keep to these rules, and one draw needn't show every extreme that they name: `pre_variate`: each variate's tokens form one run of at most 128 positions. `dec_len`: some request has exactly 1023 cached tokens. `dec_table`: entries past a request's last page are unused; requests may share pages. `dec_holder`: among the 16 requests of one column group at most 2 name the same holder, a bound that some block reaches of them.
All inputs are finite; a program needn't handle non-finite values. No bound on the sum of `pre_keep` on one device may be relied on, other than what follows from the above.
Results may differ from a plain program's by a relative error of at most 0.015.
Values may be sent and summed in bfloat16 or wider, within the bound.
No kernel may reach another device: no remote copies, remote signals or barrier semaphores. Data moves between devices by JAX's collectives and lax.ppermute only.
A program may use at most 128 MiB of HBM per device.

v0:
```python
import jax
import jax.numpy as jnp
from jax import lax
from jax.sharding import PartitionSpec as P

HD = 64
eps = 1e-05


def as_sent(array):
    return jax.tree.map(lambda a: a.astype(jnp.bfloat16) if a.dtype == jnp.float32 else a, array)


def norm_rows(values, gain_row):
    return values * lax.rsqrt(jnp.mean(values * values, axis=-1, keepdims=True) + eps) * gain_row


def rotate(tensor, places):
    half_size = tensor.shape[-1] // 2
    spacing = jnp.arange(half_size).astype(jnp.float32) * (2.0 / tensor.shape[-1])
    angles = places.astype(jnp.float32)[:, None] * jnp.power(10000.0, -spacing)[None, :]
    cosine = jnp.cos(angles)[:, None, :]
    sine_part = jnp.sin(angles)[:, None, :]
    lower_half = tensor[..., :half_size]
    upper_half = tensor[..., half_size:]
    return jnp.concatenate(
        [
            lower_half * cosine - upper_half * sine_part,
            upper_half * cosine + lower_half * sine_part,
        ],
        axis=-1,
    )


def segment_time(variates):
    places = jnp.arange(variates.shape[0])
    run_start = jnp.concatenate([jnp.ones((1,), dtype=jnp.bool_), variates[1:] != variates[:-1]])
    starts = lax.cummax(jnp.where(run_start, places, 0), axis=0)
    return places - starts


def on_device(
    layer_input,
    w_q,
    w_k,
    w_v,
    w_o,
    w_gate,
    w_up,
    w_down,
    norm1,
    norm2,
    q_gain,
    k_gain,
    bias_same,
    bias_diff,
    pre_variate,
    pre_keep,
    dec_variate,
    dec_len,
    dec_table,
    dec_holder,
    kv_pool,
    page_variates,
):
    row_count = layer_input.shape[0]
    local_width = layer_input.shape[1]
    pre_len = pre_variate.shape[1]
    dec_count = dec_len.shape[0]
    heads_here = local_width // HD
    score_scale = HD ** (-0.5)
    page_size = kv_pool.shape[2]
    page_count = dec_table.shape[1]
    gathered_input = lax.all_gather(layer_input, "row", axis=1, tiled=True)
    normed = norm_rows(gathered_input.astype(jnp.float32), norm1).astype(jnp.bfloat16)
    pieces = (
        lax.all_gather(w_q, "col", axis=0, tiled=True),
        lax.all_gather(w_k, "col", axis=0, tiled=True),
        lax.all_gather(w_v, "col", axis=0, tiled=True),
    )
    columns = normed
    queries = jnp.dot(columns, pieces[0], preferred_element_type=jnp.float32)
    keys_proj = jnp.dot(columns, pieces[1], preferred_element_type=jnp.float32)
    values_proj = jnp.dot(columns, pieces[2], preferred_element_type=jnp.float32)
    places = jnp.concatenate([segment_time(pre_variate[0]), dec_len])
    query_rot = rotate(
        norm_rows(queries.reshape(row_count, heads_here, HD), q_gain.reshape(heads_here, HD)),
        places,
    ).astype(jnp.bfloat16)
    key_rot = rotate(
        norm_rows(keys_proj.reshape(row_count, heads_here, HD), k_gain.reshape(heads_here, HD)),
        places,
    ).astype(jnp.bfloat16)
    value_bf = values_proj.astype(jnp.bfloat16).reshape(row_count, heads_here, HD)

    def attend_slot(inputs):
        float_item, int_item = inputs
        new_query = float_item[:local_width].reshape(heads_here, HD)
        new_key = float_item[local_width : 2 * local_width]
        new_value = float_item[2 * local_width :]
        page_rows = int_item[:page_count]
        length = int_item[page_count]
        variate = int_item[page_count + 1]
        gathered = kv_pool[page_rows]
        cached_keys = gathered[:, 0].reshape(page_count * page_size, heads_here, HD)
        cached_vals = gathered[:, 1].reshape(page_count * page_size, heads_here, HD)
        key_variates = page_variates[page_rows].reshape(page_count * page_size)
        scores = (
            jnp.einsum("hd,khd->hk", new_query, cached_keys, preferred_element_type=jnp.float32)
            * score_scale
        )
        scores = scores + jnp.where(
            (key_variates == variate)[None, :], bias_same[:, None], bias_diff[:, None]
        )
        key_heads = new_key.reshape(heads_here, HD)
        value_heads = new_value.reshape(heads_here, HD)
        own_score = (
            jnp.sum(new_query.astype(jnp.float32) * key_heads.astype(jnp.float32), axis=1)
            * score_scale
            + bias_same
        )
        exp_scores = jnp.where(
            (jnp.arange(page_count * page_size) < length)[None, :], jnp.exp(scores), 0.0
        )
        own_exp = jnp.exp(own_score)
        total_weight = jnp.sum(exp_scores, axis=1) + own_exp
        weights_bf = (exp_scores / total_weight[:, None]).astype(jnp.bfloat16)
        own_weight = (own_exp / total_weight).astype(jnp.bfloat16)
        attended = jnp.einsum(
            "hk,khd->hd", weights_bf, cached_vals, preferred_element_type=jnp.float32
        ) + own_weight.astype(jnp.float32)[:, None] * value_heads.astype(jnp.float32)
        tail_slot = page_rows[length // page_size]
        old_page = kv_pool[tail_slot]
        hit_row = (jnp.arange(page_size) == length % page_size)[None, :, None]
        new_rows = jnp.stack([new_key, new_value])[:, None, :]
        return (
            attended.astype(jnp.bfloat16).reshape(local_width),
            jnp.where(hit_row, new_rows, old_page),
        )

    keep_mask = pre_keep[0]
    variates = pre_variate[0]
    block_rows = min(512, pre_len)
    pre_keys = key_rot[:pre_len]
    pre_values = value_bf[:pre_len]
    block_queries = query_rot[0:block_rows]
    scores = (
        jnp.einsum("qhd,khd->hqk", block_queries, pre_keys, preferred_element_type=jnp.float32)
        * score_scale
    )
    same_var = variates[0:block_rows, None] == variates[None, :]
    scores = scores + jnp.where(same_var[None], bias_same[:, None, None], bias_diff[:, None, None])
    allowed = (keep_mask[None, :] == 1) | (
        jnp.arange(0, block_rows)[:, None] == jnp.arange(pre_len)[None, :]
    )
    exp_scores = jnp.where(allowed[None], jnp.exp(scores), 0.0)
    weights_bf = (exp_scores / jnp.sum(exp_scores, axis=2, keepdims=True)).astype(jnp.bfloat16)
    outputs = jnp.einsum(
        "hqk,khd->qhd", weights_bf, pre_values, preferred_element_type=jnp.float32
    ).astype(jnp.bfloat16)
    prefill_out = outputs.reshape(pre_len, local_width)
    peer_count = lax.axis_size("col")
    slot_count = max(2, (dec_count + peer_count - 1) // peer_count)
    holder = dec_holder[:, 0]
    onehot = (holder[:, None] == jnp.arange(peer_count)[None, :]).astype(jnp.int32)
    slot_rank = jnp.sum((jnp.cumsum(onehot, axis=0) - onehot) * onehot, axis=1)
    target = holder * slot_count + slot_rank
    payload = jnp.concatenate(
        [
            query_rot[pre_len:].reshape(dec_count, local_width),
            key_rot[pre_len:].reshape(dec_count, local_width),
            value_bf[pre_len:].reshape(dec_count, local_width),
        ],
        axis=1,
    )
    int_facts = jnp.concatenate([dec_table, dec_len[:, None], dec_variate[:, None]], axis=1)
    send_float = (
        jnp.zeros((peer_count * slot_count, 3 * local_width), jnp.bfloat16).at[target].set(payload)
    )
    send_int = (
        jnp.zeros((peer_count * slot_count, page_count + 2), jnp.int32).at[target].set(int_facts)
    )
    send_float = send_float.reshape(peer_count, slot_count, 3 * local_width)
    send_int = send_int.reshape(peer_count, slot_count, page_count + 2)
    floats = lax.all_to_all(send_float, "col", split_axis=0, concat_axis=0, tiled=True)
    int_part = lax.all_to_all(send_int, "col", split_axis=0, concat_axis=0, tiled=True)
    group_count = floats.shape[0]
    item_count = floats.shape[1]
    flat_floats = floats.reshape(group_count * item_count, floats.shape[2])
    flat_ints = int_part.reshape(group_count * item_count, int_part.shape[2])
    batch_slots = min(16, group_count * item_count)
    slot_out, slot_tail = lax.map(attend_slot, (flat_floats, flat_ints), batch_size=batch_slots)
    slot_out = slot_out.reshape(group_count, item_count, local_width)
    slot_tail = slot_tail.reshape(group_count, item_count, 2, page_size, local_width)
    back_out = lax.all_to_all(
        as_sent(slot_out), "col", split_axis=0, concat_axis=0, tiled=True
    ).astype(slot_out.dtype)
    back_tail = lax.all_to_all(
        as_sent(slot_tail), "col", split_axis=0, concat_axis=0, tiled=True
    ).astype(slot_tail.dtype)
    decode_out = back_out.reshape(peer_count * slot_count, local_width)[target]
    tails = back_tail.reshape(peer_count * slot_count, 2, page_size, local_width)[target]
    decode_out, tail_pages = (decode_out, tails)
    all_attended = jnp.concatenate([prefill_out, decode_out], axis=0)
    partial_out = jnp.dot(
        all_attended,
        lax.all_gather(w_o, "col", axis=1, tiled=True),
        preferred_element_type=jnp.float32,
    )
    share_start = lax.axis_index("row") * local_width
    attn_total = lax.psum(partial_out.astype(jnp.bfloat16), "row").astype(jnp.float32)
    resid_full = gathered_input.astype(jnp.float32) + attn_total
    ffn_input = norm_rows(resid_full, norm2).astype(jnp.bfloat16)
    resid_share = lax.dynamic_slice_in_dim(resid_full, share_start, local_width, 1)
    zero_hidden = jnp.zeros((row_count, w_gate.shape[1]), jnp.float32)
    pieces = (
        lax.all_gather(w_gate, "col", axis=0, tiled=True),
        lax.all_gather(w_up, "col", axis=0, tiled=True),
    )
    columns = lax.slice_in_dim(ffn_input, 0, pieces[0].shape[0], axis=1)
    gate_proj = zero_hidden + jnp.dot(columns, pieces[0], preferred_element_type=jnp.float32)
    up_proj = zero_hidden + jnp.dot(columns, pieces[1], preferred_element_type=jnp.float32)
    hidden_units = (jax.nn.silu(gate_proj) * up_proj).astype(jnp.bfloat16)
    partial_ffn = jnp.dot(
        hidden_units,
        lax.all_gather(w_down, "col", axis=1, tiled=True),
        preferred_element_type=jnp.float32,
    )
    ffn_share = lax.psum_scatter(
        partial_ffn.astype(jnp.bfloat16), "row", scatter_dimension=1, tiled=True
    ).astype(jnp.float32)
    hidden = (resid_share + ffn_share).astype(jnp.bfloat16)
    prefill_pages = jnp.stack(
        [
            key_rot[:pre_len].reshape(pre_len // page_size, page_size, local_width),
            value_bf[:pre_len].reshape(pre_len // page_size, page_size, local_width),
        ],
        axis=1,
    )
    return (hidden, prefill_pages, tail_pages)


def solution(mesh):
    placed = (
        P("col", "row"),
        P("col", "row"),
        P("col", "row"),
        P("col", "row"),
        P("row", "col"),
        P("col", "row"),
        P("col", "row"),
        P("row", "col"),
        P(),
        P(),
        P("row"),
        P("row"),
        P("row"),
        P("row"),
        P("col", None),
        P("col", None),
        P("col"),
        P("col"),
        P("col", None),
        P("col", None),
        P("col", None, None, "row"),
        P("col", None),
    )
    return jax.shard_map(
        on_device,
        mesh=mesh,
        in_specs=placed,
        out_specs=(P("col", "row"), P("col", None, None, "row"), P("col", None, None, "row")),
        check_vma=False,
    )
```

profile of v0, /device:TPU:8, one launch (start us, length us, event | category | flops | bytes accessed | tf_op | source)
XLA Modules:
  0.0 774.8 jit_solution(16630199738598560226)
XLA Ops:
  15.8 51.9 %all_gather.27 = bf16[1024,128]{1,0:T(8,128)(2,1)S(1)} all-gather(bf16[32,128]{1,0:T(8,128)(2,1)} %param.26), channel_id=1, replica_groups=mesh['row'=8,'col'=32] {'col'}, dimensions={0}, use_global_device_ids=true | all-gather | bytes 270336 | tf_op jit(solution)/shard_map/all_gather | solution.py:78
  67.7 47.2 %all_gather.26 = bf16[1024,128]{1,0:T(8,128)(2,1)S(1)} all-gather(bf16[32,128]{1,0:T(8,128)(2,1)} %param.25), channel_id=1, replica_groups=mesh['row'=8,'col'=32] {'col'}, dimensions={0}, use_global_device_ids=true | all-gather | bytes 270336 | tf_op jit(solution)/shard_map/all_gather | solution.py:77
  114.9 47.7 %all_gather.25 = bf16[1024,128]{1,0:T(8,128)(2,1)S(1)} all-gather(bf16[32,128]{1,0:T(8,128)(2,1)} %param.27), channel_id=1, replica_groups=mesh['row'=8,'col'=32] {'col'}, dimensions={0}, use_global_device_ids=true | all-gather | bytes 270336 | tf_op jit(solution)/shard_map/all_gather | solution.py:79
  162.6 51.4 %all_gather.28 = bf16[128,1024]{0,1:T(8,128)(2,1)} all-gather(bf16[128,32]{0,1:T(8,128)(2,1)} %param.28), channel_id=1, replica_groups=mesh['row'=8,'col'=32] {'col'}, dimensions={1}, use_global_device_ids=true | all-gather | bytes 270336 | tf_op jit(solution)/shard_map/all_gather | solution.py:207
  223.5 7.1 all-to-all-start.1
  230.6 8.7 %all-to-all-done.1 = bf16[32,2,384]{2,1,0:T(2,128)(2,1)S(1)} async-done(((bf16[32,2,384]{2,1,0:T(2,128)(2,1)}), bf16[32,2,384]{2,1,0:T(2,128)(2,1)S(1)}, u32[]{:S(2)}, u32[]{:S(2)}) %all-to-all-start.1) | async-done | bytes 49184 | tf_op jit(solution)/shard_map/all_to_all | solution.py:185
  253.0 209.6 %while.14 = (s32[]{:T(128)}, bf16[4,16,128]{2,1,0:T(8,128)(2,1)}, bf16[4,16,2,128,128]{4,3,2,1,0:T(8,128)(2,1)}, s32[4,16,10]{2,1,0:T(8,128)S(1)}, bf16[4,16,384...) while((s32[]{:T(128)}, bf16[4,16,128]{2,1,0:T(8,128)(2,1)}, ...), condition=%wide.region_13.14_spmd, body=%wide.region_10.13_spmd.sunk | while | flops 9330754 | bytes 80879120 | solution.py:192
  254.0 6.4 gather_fusion
  266.5 6.7 copy.139
  273.3 7.3 squeeze.36
  284.3 6.7 copy.137
  291.0 7.3 squeeze.35
  306.5 6.4 gather_fusion
  319.0 6.7 copy.139
  325.7 7.3 squeeze.36
  336.7 6.7 copy.137
  343.5 7.3 squeeze.35
  371.4 6.7 copy.139
  378.1 7.3 squeeze.36
  389.1 6.7 copy.137
  395.8 7.3 squeeze.35
  423.7 6.7 copy.139
  430.4 7.3 squeeze.36
  441.4 6.7 copy.137
  448.1 7.3 squeeze.35
  470.4 6.9 all-to-all-done.2
  480.2 6.8 all-to-all-start.3
  488.4 58.4 %all-reduce.2.cloned.1.call-done = bf16[528,1024]{1,0:T(8,128)(2,1)} async-done(((bf16[528,1024]{1,0:T(8,128)(2,1)}), bf16[528,1024]{1,0:T(8,128)(2,1)}) %all-reduce.2.cloned.1.call-update) | async-done | bytes 1081360 | tf_op jit(solution)/shard_map/psum | solution.py:211
  548.5 19.2 %all-gather.7.cloned.1.call-done = bf16[1024,512]{1,0:T(8,128)(2,1)} async-done(((bf16[32,512]{1,0:T(8,128)(2,1)}), bf16[1024,512]{1,0:T(8,128)(2,1)}) %all-gather.7.cloned.1.call-update) | async-done | bytes 1048592 | tf_op jit(solution)/shard_map/all_gather | solution.py:217
  571.0 73.5 %all-gather.11.cloned.1.call-done = bf16[512,1024]{0,1:T(8,128)(2,1)} async-done(((bf16[512,32]{0,1:T(8,128)(2,1)}), bf16[512,1024]{0,1:T(8,128)(2,1)}) %all-gather.11.cloned.1.call-update) | async-done | bytes 1048592 | tf_op jit(solution)/shard_map/all_gather | solution.py:226
  644.5 76.8 %all-gather.9.cloned.1.call-done = bf16[1024,512]{1,0:T(8,128)(2,1)} async-done(((bf16[32,512]{1,0:T(8,128)(2,1)}), bf16[1024,512]{1,0:T(8,128)(2,1)}) %all-gather.9.cloned.1.call-update) | async-done | bytes 1048592 | tf_op jit(solution)/shard_map/all_gather | solution.py:218
  729.3 32.6 %reduce-scatter.4.cloned.1.call-done = bf16[128,528]{1,0:T(8,128)(2,1)} async-done(((bf16[1024,528]{1,0:T(8,128)(2,1)}), bf16[128,528]{1,0:T(8,128)(2,1)}) %reduce-scatter.4.cloned.1.call-update) | async-done | bytes 135184
  (241 shorter events, 145.5 us)
Async XLA Ops:
  8.0 210.7 %copy-start.7 = (f32[1024]{0:T(1024)S(1)}, f32[1024]{0:T(1024)}, u32[]{:S(2)}) copy-start(f32[1024]{0:T(1024)} %param.32) | copy-start | bytes 12292
  8.0 209.0 %all-gather.5.cloned.1.call-start = ((), (), s32[]{:S(2)}) async-start(), calls=%async_computation.5 | async-start | bytes 1216512 | tf_op jit(solution)/shard_map/all_gather | solution.py:74
  217.0 3.5 copy-start.2
  221.4 22.9 %copy-start.5 = (f32[2]{0:T(128)S(1)}, f32[2]{0:T(128)}, u32[]{:S(2)}) copy-start(f32[2]{0:T(128)} %param.36) | copy-start | bytes 28
  221.4 22.9 %copy-start.6 = (f32[2]{0:T(128)S(1)}, f32[2]{0:T(128)}, u32[]{:S(2)}) copy-start(f32[2]{0:T(128)} %param.37) | copy-start | bytes 28
  223.5 15.8 %all-to-all-start.1 = ((bf16[32,2,384]{2,1,0:T(2,128)(2,1)}), bf16[32,2,384]{2,1,0:T(2,128)(2,1)S(1)}, u32[]{:S(2)}, u32[]{:S(2)}) async-start(bf16[32,2,384]{2,1,0:T(2,128)(2,1)} %reshape.400), calls=%async_computation.1 | async-start | bytes 98304 | tf_op jit(solution)/shard_map/all_to_all | solution.py:185
  239.3 13.7 %all-to-all-start = ((s32[32,2,10]{2,1,0:T(2,128)}), s32[32,2,10]{2,1,0:T(2,128)S(1)}, u32[]{:S(2)}, u32[]{:S(2)}) async-start(s32[32,2,10]{2,1,0:T(2,128)} %bitcast.30), calls=%async_computation | async-start | bytes 65536 | tf_op jit(solution)/shard_map/all_to_all | solution.py:186
  244.3 8.7 %copy-start = (bf16[32,2,128,128]{3,2,1,0:T(8,128)(2,1)S(1)}, bf16[32,2,128,128]{3,2,1,0:T(8,128)(2,1)}, u32[]{:S(2)}) copy-start(bf16[32,2,128,128]{3,2,1,0:T(8,128)(2,1)} %param.44) | copy-start | bytes 6291460
  244.3 8.7 %copy-start.1 = (s32[32,128]{1,0:T(8,128)S(1)}, s32[32,128]{1,0:T(8,128)}, u32[]{:S(2)}) copy-start(s32[32,128]{1,0:T(8,128)} %param.45) | copy-start | bytes 49156
  462.5 14.8 %all-to-all-start.2 = ((bf16[32,2,128]{2,1,0:T(2,128)(2,1)}), bf16[32,2,128]{2,1,0:T(2,128)(2,1)S(1)}, u32[]{:S(2)}, u32[]{:S(2)}) async-start(bf16[32,2,128]{2,1,0:T(2,128)(2,1)} %bitcast.34), calls=%async_computation.2 | async-start | bytes 32768 | tf_op jit(solution)/shard_map/all_to_all | solution.py:195
  467.6 79.2 %all-reduce.2.cloned.1.call-start = ((), (), s32[]{:S(2)}) async-start(), calls=%async_computation.6 | async-start | bytes 2162688 | tf_op jit(solution)/shard_map/psum | solution.py:211
  467.7 10.4 %copy-start.4 = (bf16[128,1024]{0,1:T(8,128)(2,1)S(1)}, bf16[128,1024]{0,1:T(8,128)(2,1)}, u32[]{:S(2)}) copy-start(bf16[128,1024]{0,1:T(8,128)(2,1)} %all_gather.28) | copy-start | bytes 786436
  479.6 88.1 %all-gather.7.cloned.1.call-start = ((), (), s32[]{:S(2)}) async-start(), calls=%async_computation.7 | async-start | bytes 1081344 | tf_op jit(solution)/shard_map/all_gather | solution.py:217
  480.2 66.7 %copy-start.3 = (bf16[528,1024]{1,0:T(8,128)(2,1)S(1)}, bf16[528,1024]{1,0:T(8,128)(2,1)}, u32[]{:S(2)}) copy-start(bf16[528,1024]{1,0:T(8,128)(2,1)} %all-gather.5.cloned.1.call-done) | copy-start | bytes 3244036
  480.2 283.5 %all-to-all-start.3 = ((bf16[32,2,2,128,128]{4,3,2,1,0:T(8,128)(2,1)}), bf16[32,2,2,128,128]{4,3,2,1,0:T(8,128)(2,1)}, u32[]{:S(2)}, u32[]{:S(2)}) async-start(bf16[32,2,2,128,128]{4,3,2,1,0:T(8,128)(2,1)} %bitcast.142), calls=%async_computation.3 | async-start | bytes 8388608 | tf_op jit(solution)/shard_map/all_to_all | solution.py:198
  487.0 157.5 %all-gather.11.cloned.1.call-start = ((), (), s32[]{:S(2)}) async-start(), calls=%async_computation.9 | async-start | bytes 1081344 | tf_op jit(solution)/shard_map/all_gather | solution.py:226
  487.6 233.7 %all-gather.9.cloned.1.call-start = ((), (), s32[]{:S(2)}) async-start(), calls=%async_computation.8 | async-start | bytes 1081344 | tf_op jit(solution)/shard_map/all_gather | solution.py:218
  488.1 79.6 %copy-start.8 = (f32[1024]{0:T(1024)S(1)}, f32[1024]{0:T(1024)}, u32[]{:S(2)}) copy-start(f32[1024]{0:T(1024)} %param.33) | copy-start | bytes 12292
  488.1 273.8 %reduce-scatter.4.cloned.1.call-start = ((), (), s32[]{:S(2)}) async-start(), calls=%async_computation.10 | async-start | bytes 1474560
Sparse Core Ops, SparseCore 0:
  10.7 28.8 all-gather.4
  479.7 67.0 all-reduce.1
  728.5 33.3 reduce-scatter.3
Sparse Core Ops, SparseCore 1:
  483.0 84.7 all-gather.6
  570.5 73.9 all-gather.10
  647.3 74.0 all-gather.8
where the time goes:
time: 778 us; the launch traced here: 775 us
  waiting for transfers between devices  284 us (37%)
  blocking collectives  198 us (25%)
  local copies, waits for them, and re-layouts  189 us (24%)
  matrix products  42.3 us (5%)
  starting transfers between devices  24.4 us (3%)
  other arithmetic  21.1 us (3%)
  between operations  15.7 us (2%)
    all_gather x1, waiting for transfers between devices, on_device(): lax.all_gather(w_up, 'col', axis=0, tiled=True)  76.8 us
    all_gather x1, waiting for transfers between devices, on_device(): lax.all_gather(w_down, 'col', axis=1, tiled=True)  73.5 us
    psum x1, waiting for transfers between devices, on_device(): lax.psum(partial_out.astype(jnp.bfloat16), 'row').astype(jnp.float32)  58.4 us
    while x8, local copies, waits for them, and re-layouts  53.9 us
    all_gather x1, blocking collectives, on_device(): lax.all_gather(w_k, 'col', axis=0, tiled=True)  51.9 us
    all_gather x1, blocking collectives, on_device(): lax.all_gather(w_o, 'col', axis=1, tiled=True)  51.4 us
    all_gather x1, blocking collectives, on_device(): lax.all_gather(w_v, 'col', axis=0, tiled=True)  47.7 us
    all_gather x1, blocking collectives, on_device(): lax.all_gather(w_q, 'col', axis=0, tiled=True)  47.2 us
  transfers between devices with their start and end apart: 10, of which 8 were waited for; matrix products, arithmetic and copies ran while one was open for 4% of the time, Pallas kernels for 0%

commit v1 on v0

--- a/solution.py
+++ b/solution.py
@@ -208,7 +208,9 @@
         preferred_element_type=jnp.float32,
     )
     share_start = lax.axis_index("row") * local_width
-    attn_total = lax.psum(partial_out.astype(jnp.bfloat16), "row").astype(jnp.float32)
+    attn_total = jnp.sum(lax.all_gather(partial_out.astype(jnp.bfloat16), "row"), axis=0).astype(
+        jnp.float32
+    )
     resid_full = gathered_input.astype(jnp.float32) + attn_total
     ffn_input = norm_rows(resid_full, norm2).astype(jnp.bfloat16)
     resid_share = lax.dynamic_slice_in_dim(resid_full, share_start, local_width, 1)

time: 778 us -> 814 us (1.046)
  waiting for transfers between devices: 284 us -> 315 us
    psum x1 -> x0, waiting for transfers between devices: 58.4 us -> none  [on_device(): lax.psum(partial_out.astype(jnp.bfloat16), 'row').astype(jnp.float32)]
    all_gather x1, waiting for transfers between devices: 19.2 us -> 70.4 us  [on_device(): lax.all_gather(w_gate, 'col', axis=0, tiled=True)]
    all_gather x0 -> x1, waiting for transfers between devices: none -> 42.5 us  [on_device(): lax.all_gather(partial_out.astype(jnp.bfloat16), 'row')]
  transfers between devices with their start and end apart: 10 -> 10, of which waited for: 8 -> 8; matrix products, arithmetic and copies ran while one was open for 4% -> 5% of each run, Pallas kernels for 0% -> 0%
where the time goes in v1:
time: 814 us; the launch traced here: 811 us
  waiting for transfers between devices  315 us (39%)
  blocking collectives  198 us (24%)
  local copies, waits for them, and re-layouts  189 us (23%)
  matrix products  41.6 us (5%)
  other arithmetic  28 us (3%)
  starting transfers between devices  24.5 us (3%)
  between operations  14.4 us (2%)
    all_gather x1, waiting for transfers between devices, on_device(): lax.all_gather(w_down, 'col', axis=1, tiled=True)  76.3 us
    all_gather x1, waiting for transfers between devices, on_device(): lax.all_gather(w_up, 'col', axis=0, tiled=True)  73.3 us
    all_gather x1, waiting for transfers between devices, on_device(): lax.all_gather(w_gate, 'col', axis=0, tiled=True)  70.4 us
    while x8, local copies, waits for them, and re-layouts  53.9 us
    all_gather x1, blocking collectives, on_device(): lax.all_gather(w_k, 'col', axis=0, tiled=True)  51.9 us
    all_gather x1, blocking collectives, on_device(): lax.all_gather(w_o, 'col', axis=1, tiled=True)  51.3 us
    all_gather x1, blocking collectives, on_device(): lax.all_gather(w_v, 'col', axis=0, tiled=True)  47.7 us
    all_gather x1, blocking collectives, on_device(): lax.all_gather(w_q, 'col', axis=0, tiled=True)  47.2 us
  transfers between devices with their start and end apart: 10, of which 8 were waited for; matrix products, arithmetic and copies ran while one was open for 5% of the time, Pallas kernels for 0%

profile of v1, /device:TPU:8, one launch (start us, length us, event | category | flops | bytes accessed | tf_op | source)
XLA Modules:
  0.0 810.7 jit_solution(4915879611112641805)
XLA Ops:
  15.0 51.9 %all_gather.33 = bf16[1024,128]{1,0:T(8,128)(2,1)S(1)} all-gather(bf16[32,128]{1,0:T(8,128)(2,1)} %param.26), channel_id=1, replica_groups=mesh['row'=8,'col'=32] {'col'}, dimensions={0}, use_global_device_ids=true | all-gather | bytes 270336 | tf_op jit(solution)/shard_map/all_gather | solution.py:78
  66.9 47.2 %all_gather.32 = bf16[1024,128]{1,0:T(8,128)(2,1)S(1)} all-gather(bf16[32,128]{1,0:T(8,128)(2,1)} %param.25), channel_id=1, replica_groups=mesh['row'=8,'col'=32] {'col'}, dimensions={0}, use_global_device_ids=true | all-gather | bytes 270336 | tf_op jit(solution)/shard_map/all_gather | solution.py:77
  114.1 47.7 %all_gather.31 = bf16[1024,128]{1,0:T(8,128)(2,1)S(1)} all-gather(bf16[32,128]{1,0:T(8,128)(2,1)} %param.27), channel_id=1, replica_groups=mesh['row'=8,'col'=32] {'col'}, dimensions={0}, use_global_device_ids=true | all-gather | bytes 270336 | tf_op jit(solution)/shard_map/all_gather | solution.py:79
  161.7 51.3 %all_gather.34 = bf16[128,1024]{0,1:T(8,128)(2,1)} all-gather(bf16[128,32]{0,1:T(8,128)(2,1)} %param.28), channel_id=1, replica_groups=mesh['row'=8,'col'=32] {'col'}, dimensions={1}, use_global_device_ids=true | all-gather | bytes 270336 | tf_op jit(solution)/shard_map/all_gather | solution.py:207
  222.5 7.3 all-to-all-start.1
  229.9 8.7 %all-to-all-done.1 = bf16[32,2,384]{2,1,0:T(2,128)(2,1)S(1)} async-done(((bf16[32,2,384]{2,1,0:T(2,128)(2,1)}), bf16[32,2,384]{2,1,0:T(2,128)(2,1)S(1)}, u32[]{:S(2)}, u32[]{:S(2)}) %all-to-all-start.1) | async-done | bytes 49184 | tf_op jit(solution)/shard_map/all_to_all | solution.py:185
  252.2 209.7 %while.14 = (s32[]{:T(128)}, bf16[4,16,128]{2,1,0:T(8,128)(2,1)}, bf16[4,16,2,128,128]{4,3,2,1,0:T(8,128)(2,1)}, s32[4,16,10]{2,1,0:T(8,128)S(1)}, bf16[4,16,384...) while((s32[]{:T(128)}, bf16[4,16,128]{2,1,0:T(8,128)(2,1)}, ...), condition=%wide.region_13.14_spmd, body=%wide.region_10.13_spmd.sunk | while | flops 9330754 | bytes 80879120 | solution.py:192
  253.3 6.4 gather_fusion
  265.8 6.7 copy.139
  272.6 7.3 squeeze.36
  283.6 6.7 copy.137
  290.3 7.3 squeeze.35
  305.8 6.4 gather_fusion
  318.3 6.7 copy.139
  325.0 7.3 squeeze.36
  336.0 6.7 copy.137
  342.8 7.3 squeeze.35
  370.7 6.7 copy.139
  377.4 7.3 squeeze.36
  388.4 6.7 copy.137
  395.1 7.3 squeeze.35
  423.1 6.7 copy.139
  429.8 7.3 squeeze.36
  440.8 6.7 copy.137
  447.5 7.3 squeeze.35
  469.8 6.9 all-to-all-done.2
  479.7 6.7 all-to-all-start.3
  487.7 42.5 %all-gather.15.cloned.1.call-done = bf16[4224,1024]{1,0:T(8,128)(2,1)} async-done(((bf16[528,1024]{1,0:T(8,128)(2,1)}), bf16[4224,1024]{1,0:T(8,128)(2,1)}) %all-gather.15.cloned.1.call-update) | async-done | bytes 8650768 | tf_op jit(solution)/shard_map/all_gather | solution.py:211
  537.9 70.4 %all-gather.9.cloned.1.call-done = bf16[1024,512]{1,0:T(8,128)(2,1)} async-done(((bf16[32,512]{1,0:T(8,128)(2,1)}), bf16[1024,512]{1,0:T(8,128)(2,1)}) %all-gather.9.cloned.1.call-update) | async-done | bytes 1048592 | tf_op jit(solution)/shard_map/all_gather | solution.py:219
  611.3 73.3 %all-gather.11.cloned.1.call-done = bf16[1024,512]{1,0:T(8,128)(2,1)} async-done(((bf16[32,512]{1,0:T(8,128)(2,1)}), bf16[1024,512]{1,0:T(8,128)(2,1)}) %all-gather.11.cloned.1.call-update) | async-done | bytes 1048592 | tf_op jit(solution)/shard_map/all_gather | solution.py:220
  684.6 76.3 %all-gather.13.cloned.1.call-done = bf16[512,1024]{0,1:T(8,128)(2,1)} async-done(((bf16[512,32]{0,1:T(8,128)(2,1)}), bf16[512,1024]{0,1:T(8,128)(2,1)}) %all-gather.13.cloned.1.call-update) | async-done | bytes 1048592 | tf_op jit(solution)/shard_map/all_gather | solution.py:228
  772.4 28.8 %reduce-scatter.4.cloned.1.call-done = bf16[128,528]{1,0:T(8,128)(2,1)} async-done(((bf16[1024,528]{1,0:T(8,128)(2,1)}), bf16[128,528]{1,0:T(8,128)(2,1)}) %reduce-scatter.4.cloned.1.call-update) | async-done | bytes 135184
  (242 shorter events, 152.0 us)
Async XLA Ops:
  7.2 210.5 %copy-start.7 = (f32[1024]{0:T(1024)S(1)}, f32[1024]{0:T(1024)}, u32[]{:S(2)}) copy-start(f32[1024]{0:T(1024)} %param.32) | copy-start | bytes 12292
  7.2 208.9 %all-gather.7.cloned.1.call-start = ((), (), s32[]{:S(2)}) async-start(), calls=%async_computation.5 | async-start | bytes 1216512 | tf_op jit(solution)/shard_map/all_gather | solution.py:74
  216.0 3.5 copy-start.2
  220.4 23.1 %copy-start.5 = (f32[2]{0:T(128)S(1)}, f32[2]{0:T(128)}, u32[]{:S(2)}) copy-start(f32[2]{0:T(128)} %param.36) | copy-start | bytes 28
  220.4 23.1 %copy-start.6 = (f32[2]{0:T(128)S(1)}, f32[2]{0:T(128)}, u32[]{:S(2)}) copy-start(f32[2]{0:T(128)} %param.37) | copy-start | bytes 28
  222.5 16.0 %all-to-all-start.1 = ((bf16[32,2,384]{2,1,0:T(2,128)(2,1)}), bf16[32,2,384]{2,1,0:T(2,128)(2,1)S(1)}, u32[]{:S(2)}, u32[]{:S(2)}) async-start(bf16[32,2,384]{2,1,0:T(2,128)(2,1)} %reshape.400), calls=%async_computation.1 | async-start | bytes 98304 | tf_op jit(solution)/shard_map/all_to_all | solution.py:185
  238.5 13.7 %all-to-all-start = ((s32[32,2,10]{2,1,0:T(2,128)}), s32[32,2,10]{2,1,0:T(2,128)S(1)}, u32[]{:S(2)}, u32[]{:S(2)}) async-start(s32[32,2,10]{2,1,0:T(2,128)} %bitcast.30), calls=%async_computation | async-start | bytes 65536 | tf_op jit(solution)/shard_map/all_to_all | solution.py:186
  243.5 8.7 %copy-start = (bf16[32,2,128,128]{3,2,1,0:T(8,128)(2,1)S(1)}, bf16[32,2,128,128]{3,2,1,0:T(8,128)(2,1)}, u32[]{:S(2)}) copy-start(bf16[32,2,128,128]{3,2,1,0:T(8,128)(2,1)} %param.44) | copy-start | bytes 6291460
  243.5 8.7 %copy-start.1 = (s32[32,128]{1,0:T(8,128)S(1)}, s32[32,128]{1,0:T(8,128)}, u32[]{:S(2)}) copy-start(s32[32,128]{1,0:T(8,128)} %param.45) | copy-start | bytes 49156
  461.9 14.8 %all-to-all-start.2 = ((bf16[32,2,128]{2,1,0:T(2,128)(2,1)}), bf16[32,2,128]{2,1,0:T(2,128)(2,1)S(1)}, u32[]{:S(2)}, u32[]{:S(2)}) async-start(bf16[32,2,128]{2,1,0:T(2,128)(2,1)} %bitcast.34), calls=%async_computation.2 | async-start | bytes 32768 | tf_op jit(solution)/shard_map/all_to_all | solution.py:195
  467.0 63.2 %all-gather.15.cloned.1.call-start = ((), (), s32[]{:S(2)}) async-start(), calls=%async_computation.9 | async-start | bytes 9732096 | tf_op jit(solution)/shard_map/all_gather | solution.py:211
  467.1 10.3 %copy-start.4 = (bf16[128,1024]{0,1:T(8,128)(2,1)S(1)}, bf16[128,1024]{0,1:T(8,128)(2,1)}, u32[]{:S(2)}) copy-start(bf16[128,1024]{0,1:T(8,128)(2,1)} %all_gather.34) | copy-start | bytes 786436
  478.9 129.4 %all-gather.9.cloned.1.call-start = ((), (), s32[]{:S(2)}) async-start(), calls=%async_computation.6 | async-start | bytes 1081344 | tf_op jit(solution)/shard_map/all_gather | solution.py:219
  479.7 288.9 %all-to-all-start.3 = ((bf16[32,2,2,128,128]{4,3,2,1,0:T(8,128)(2,1)}), bf16[32,2,2,128,128]{4,3,2,1,0:T(8,128)(2,1)}, u32[]{:S(2)}, u32[]{:S(2)}) async-start(bf16[32,2,2,128,128]{4,3,2,1,0:T(8,128)(2,1)} %bitcast.144), calls=%async_computation.3 | async-start | bytes 8388608 | tf_op jit(solution)/shard_map/all_to_all | solution.py:198
  486.3 198.3 %all-gather.11.cloned.1.call-start = ((), (), s32[]{:S(2)}) async-start(), calls=%async_computation.7 | async-start | bytes 1081344 | tf_op jit(solution)/shard_map/all_gather | solution.py:220
  486.9 274.0 %all-gather.13.cloned.1.call-start = ((), (), s32[]{:S(2)}) async-start(), calls=%async_computation.8 | async-start | bytes 1081344 | tf_op jit(solution)/shard_map/all_gather | solution.py:228
  487.5 313.6 %reduce-scatter.4.cloned.1.call-start = ((), (), s32[]{:S(2)}) async-start(), calls=%async_computation.10 | async-start | bytes 1474560
  530.2 5.9 copy-start.3
  536.2 72.1 %copy-start.8 = (f32[1024]{0:T(1024)S(1)}, f32[1024]{0:T(1024)}, u32[]{:S(2)}) copy-start(f32[1024]{0:T(1024)} %param.33) | copy-start | bytes 12292
Sparse Core Ops, SparseCore 0:
  9.8 28.8 all-gather.6
  479.0 51.1 all-gather.14
  532.8 75.4 all-gather.8
  610.7 73.8 all-gather.10
  687.0 73.8 all-gather.12
  767.7 33.3 reduce-scatter.3
